TPU v7x, 256 devices: a whole 4x4x8 slice. The times are simulated.
256 devices in a mesh: ctx: 32 (over x, y, core), head: 8 (over z).
Axes of the slice: x: 4, y: 4, z: 8, core: 2. Of those that a mesh axis runs over, the one named last changes fastest.
Arguments:
- queries: bfloat16 [8192, 8192], P('ctx', 'head'), may hold values from -110 to 110
- keys: bfloat16 [8192, 1024], P('ctx', 'head'), may hold values from -3.1 to 3.1
- values: bfloat16 [8192, 1024], P('ctx', 'head'), may hold values from -6 to 6
- cf_queries: bfloat16 [8192, 8192], P('ctx', 'head'), may hold values from -6 to 6
- cf_keys: bfloat16 [8192, 1024], P('ctx', 'head'), may hold values from -6 to 6
- cf_values: bfloat16 [8192, 1024], P('ctx', 'head'), may hold values from -6 to 6
- patch_source: int32 [8192], replicated, may hold values from -1 to 8191, as said below
- doc_lengths: int32 [32], replicated, may hold values from 1 to 4608, as said below
- out_weight: bfloat16 [8192, 4096], P('head'), may hold values from -0.5 to 0.5
Outputs:
- attn_out: bfloat16 [8192, 4096], P(('ctx', 'head'))
Inputs may be any that keep to these rules, and one draw needn't show every extreme that they name: `patch_source`: exactly one aligned block of 128 positions of each index of ctx is replaced; its rows come from 16 different indices of ctx, 8 consecutive rows from each; no counterfactual position is used twice. `doc_lengths`: the lengths sum to 8192, and one document has exactly 4608 positions.
All inputs are finite; a program needn't handle non-finite values.
Results may differ from a plain program's by a relative error of at most 0.014.
Values may be sent and summed in bfloat16 or wider, within the bound.
A program may use at most 192 MiB of HBM per device.

v0:
```python
import math
import jax
import jax.numpy as jnp
from jax import lax
from jax.sharding import PartitionSpec as P

HD = 128
BLK = 128


def attend_block(running, pieces, grouped, query_pos, query_doc, doc_ends):
    row_max, row_sum, weighted = running
    key_piece, value_piece = pieces
    piece_rows = key_piece.shape[0]
    kv_heads = grouped.shape[1]
    key_heads = key_piece.reshape(piece_rows, kv_heads, HD)
    value_heads = value_piece.reshape(piece_rows, kv_heads, HD)
    scores = jnp.einsum(
        "qhgd,khd->hgqk", grouped, key_heads, preferred_element_type=jnp.float32
    ) * (1.0 / math.sqrt(HD))
    key_pos = jnp.arange(piece_rows, dtype=jnp.int32)
    key_doc = jnp.sum((key_pos[:, None] >= doc_ends[None, :]).astype(jnp.int32), axis=1)
    visible = (
        (query_pos[:, None] >= key_pos[None, :])
        & (query_doc[:, None] == key_doc[None, :])
        & (key_pos[None, :] >= 0)
    )
    scores = jnp.where(visible, scores, -jnp.inf)
    new_max = jnp.max(scores, axis=-1)
    safe_max = jnp.where(new_max == -jnp.inf, 0.0, new_max)
    rescale = jnp.exp(row_max - safe_max)
    weights = jnp.exp(scores - safe_max[..., None])
    row_sum = row_sum * rescale + jnp.sum(weights, axis=-1)
    weighted = weighted * rescale[..., None] + jnp.einsum(
        "hgqk,khd->hgqd",
        weights.astype(jnp.bfloat16),
        value_heads,
        preferred_element_type=jnp.float32,
    )
    return (new_max, row_sum, weighted)


def per_device(
    queries, keys, values, cf_queries, cf_keys, cf_values, patch_source, doc_lengths, out_weight
):
    ctx_size = lax.axis_size("ctx")
    my_index = lax.axis_index("ctx")
    local_rows = queries.shape[0]
    group_count = min(ctx_size, 16)
    slot_cap = BLK // group_count
    source_grid = patch_source.reshape(ctx_size, local_rows)
    owner_dev = jnp.where(source_grid >= 0, source_grid // local_rows, -1)
    from_me = (owner_dev == my_index).astype(jnp.int32)
    slot_rank = jnp.cumsum(from_me, axis=1) - 1
    slot_index = jnp.arange(ctx_size, dtype=jnp.int32)[:, None] * slot_cap + slot_rank
    slot_index = jnp.where(from_me > 0, slot_index, ctx_size * slot_cap)
    local_source = jnp.clip(source_grid - my_index * local_rows, 0, local_rows - 1)
    send_table = (
        jnp.zeros((ctx_size * slot_cap,), jnp.int32)
        .at[slot_index.reshape(-1)]
        .set(local_source.reshape(-1), mode="drop")
    )
    send_queries = cf_queries[send_table].reshape(ctx_size, slot_cap, cf_queries.shape[1])
    send_keys = cf_keys[send_table].reshape(ctx_size, slot_cap, cf_keys.shape[1])
    send_values = cf_values[send_table].reshape(ctx_size, slot_cap, cf_values.shape[1])
    recv_queries, recv_keys, recv_values = (
        lax.all_to_all(send_queries, "ctx", split_axis=0, concat_axis=0, tiled=True),
        lax.all_to_all(send_keys, "ctx", split_axis=0, concat_axis=0, tiled=True),
        lax.all_to_all(send_values, "ctx", split_axis=0, concat_axis=0, tiled=True),
    )
    own_source = lax.dynamic_slice_in_dim(patch_source, my_index * local_rows, local_rows)
    patched = own_source >= 0
    source_dev = jnp.where(patched, own_source // local_rows, -1)
    source_hit = (source_dev[:, None] == jnp.arange(ctx_size, dtype=jnp.int32)[None, :]).astype(
        jnp.int32
    )
    earlier = jnp.cumsum(source_hit, axis=0) - source_hit
    recv_rank = jnp.sum(earlier * source_hit, axis=1)
    pick_slot = jnp.clip(source_dev * slot_cap + recv_rank, 0, ctx_size * slot_cap - 1)
    query_rows = jnp.where(
        patched[:, None], recv_queries.reshape(ctx_size * slot_cap, -1)[pick_slot], queries
    )
    key_rows = jnp.where(
        patched[:, None], recv_keys.reshape(ctx_size * slot_cap, -1)[pick_slot], keys
    )
    value_rows = jnp.where(
        patched[:, None], recv_values.reshape(ctx_size * slot_cap, -1)[pick_slot], values
    )
    kv_heads = keys.shape[1] // HD
    query_heads = queries.shape[1] // HD
    group_size = query_heads // kv_heads
    grouped = query_rows.reshape(local_rows, kv_heads, group_size, HD)
    doc_ends = jnp.cumsum(doc_lengths)
    query_pos = my_index * local_rows + jnp.arange(local_rows, dtype=jnp.int32)
    query_doc = jnp.sum((query_pos[:, None] >= doc_ends[None, :]).astype(jnp.int32), axis=1)
    initial = (
        jnp.full((kv_heads, group_size, local_rows), -jnp.inf, jnp.float32),
        jnp.zeros((kv_heads, group_size, local_rows), jnp.float32),
        jnp.zeros((kv_heads, group_size, local_rows, HD), jnp.float32),
    )
    pieces = (
        lax.all_gather(key_rows, "ctx", axis=0, tiled=True),
        lax.all_gather(value_rows, "ctx", axis=0, tiled=True),
    )
    first_row = jnp.int32(0)
    piece_rows = pieces[0].shape[0]
    last_doc = jnp.sum((first_row + piece_rows - 1 >= doc_ends).astype(jnp.int32))
    reaches = (first_row <= query_pos[local_rows - 1]) & (last_doc >= query_doc[0])

    def compute_block(previous):
        return attend_block(previous, pieces, grouped, query_pos, query_doc, doc_ends)

    def keep_block(previous):
        return previous

    running = lax.cond(reaches, compute_block, keep_block, initial)
    row_max, row_sum, weighted = running
    normalized = weighted / row_sum[..., None]
    attended = (
        jnp.transpose(normalized, (2, 0, 1, 3))
        .reshape(local_rows, query_heads * HD)
        .astype(jnp.bfloat16)
    )
    return lax.psum_scatter(
        jnp.dot(attended, out_weight, preferred_element_type=jnp.float32).astype(jnp.bfloat16),
        "head",
        scatter_dimension=0,
        tiled=True,
    )


def solution(mesh):
    in_specs = (
        P("ctx", "head"),
        P("ctx", "head"),
        P("ctx", "head"),
        P("ctx", "head"),
        P("ctx", "head"),
        P("ctx", "head"),
        P(),
        P(),
        P("head", None),
    )
    out_specs = P(("ctx", "head"), None)
    return jax.shard_map(
        per_device, mesh=mesh, in_specs=in_specs, out_specs=out_specs, check_vma=False
    )
```

profile of v0, /device:TPU:2, one launch (start us, length us, event | category | flops | bytes accessed | tf_op | source)
XLA Modules:
  0.0 307.0 jit_solution(17223273761956999939)
XLA Ops:
  9.2 30.4 %scatter_custom_fusion = s32[256]{0:T(256)S(1)} fusion(s32[8192]{0:T(1024)S(1)} %get-tuple-element.51, s32[8192]{0:T(1024)S(1)} %get-tuple-element.50, s32[]{:T(128)} %constant.69.clone.1), kind=kCustom, calls=%fused_computation.90 | custom fusion | bytes 1028 | tf_op jit(solution)/shard_map/scatter | solution.py:61
  39.7 2.2 gather_fusion.4
  41.9 7.6 %all-to-all-start.2 = ((bf16[32,8,128]{2,1,0:T(8,128)(2,1)}), bf16[32,8,128]{2,1,0:T(8,128)(2,1)S(1)}, u32[]{:S(2)}, u32[]{:S(2)}) async-start(bf16[32,8,128]{2,1,0:T(8,128)(2,1)} %bitcast.22), calls=%async_computation.2 | async-start | bytes 131072 | tf_op jit(solution)/shard_map/all_to_all | solution.py:69
  51.2 2.2 gather_fusion.2
  53.4 2.4 all-to-all-done.2
  55.8 5.0 %all-to-all-start.1 = ((bf16[32,8,128]{2,1,0:T(8,128)(2,1)}), bf16[32,8,128]{2,1,0:T(8,128)(2,1)S(1)}, u32[]{:S(2)}, u32[]{:S(2)}) async-start(bf16[32,8,128]{2,1,0:T(8,128)(2,1)} %bitcast.20), calls=%async_computation.1 | async-start | bytes 131072 | tf_op jit(solution)/shard_map/all_to_all | solution.py:68
  60.9 0.9 gather_fusion.5
  61.7 5.5 %all-to-all-done.1 = bf16[32,8,128]{2,1,0:T(8,128)(2,1)S(1)} async-done(((bf16[32,8,128]{2,1,0:T(8,128)(2,1)}), bf16[32,8,128]{2,1,0:T(8,128)(2,1)S(1)}, u32[]{:S(2)}, u32[]{:S(2)}) %all-to-all-start.1) | async-done | bytes 65568 | tf_op jit(solution)/shard_map/all_to_all | solution.py:68
  68.1 1.6 broadcast_select_fusion
  70.5 2.0 gather_fusion.1
  72.4 5.0 %all-to-all-start = ((bf16[32,8,1024]{2,1,0:T(8,128)(2,1)}), bf16[32,8,1024]{2,1,0:T(8,128)(2,1)S(1)}, u32[]{:S(2)}, u32[]{:S(2)}) async-start(bf16[32,8,1024]{2,1,0:T(8,128)(2,1)} %bitcast.16), calls=%async_computation | async-start | bytes 1048576 | tf_op jit(solution)/shard_map/all_to_all | solution.py:67
  82.5 4.8 %all-to-all-done = bf16[32,8,1024]{2,1,0:T(8,128)(2,1)S(1)} async-done(((bf16[32,8,1024]{2,1,0:T(8,128)(2,1)}), bf16[32,8,1024]{2,1,0:T(8,128)(2,1)S(1)}, u32[]{:S(2)}, u32[]{:S(2)}) %all-to-all-start) | async-done | bytes 524320 | tf_op jit(solution)/shard_map/all_to_all | solution.py:67
  87.3 31.8 %all-gather.5.cloned.1.call-done = bf16[8192,128]{1,0:T(8,128)(2,1)} async-done(((bf16[256,128]{1,0:T(8,128)(2,1)}), bf16[8192,128]{1,0:T(8,128)(2,1)}) %all-gather.5.cloned.1.call-update) | async-done | bytes 2097168 | tf_op jit(solution)/shard_map/all_gather | solution.py:103
  119.1 50.6 %all-gather.3.cloned.1.call-done = bf16[8192,128]{1,0:T(8,128)(2,1)} async-done(((bf16[256,128]{1,0:T(8,128)(2,1)}), bf16[8192,128]{1,0:T(8,128)(2,1)}) %all-gather.3.cloned.1.call-update) | async-done | bytes 2097168 | tf_op jit(solution)/shard_map/all_gather | solution.py:102
  169.7 79.6 %conditional.1 = (f32[1,8,256]{2,1,0:T(8,128)S(1)}, f32[1,8,256,128]{2,3,1,0:T(8,128)}) conditional(s32[]{:T(128)} %convert_element_type.43, () %tuple.13, (s32[256]{0:T(256)S(1)}, s32[256]{0:T(256)S(1)}, s32[32]{0:T(128)S(1)}, pred[256]{0:T(512)(128)(4,1)S(1)}, bf16[32,8,1024]{2,1,0:T(8,128)(2,1)S(1)}, /*index=5*/s32[256,1]{0,1:T(1,128)S(1)}, ...), branch_computations={%region_9.10_spmd, %region_10.14_spmd} | conditional | flops 8782093312 | bytes 219316624 | solution.py:116
  169.7 1.2 gather_fusion
  171.1 1.9 fusion.7
  173.0 25.8 %fusion.2 = (f32[8,256]{1,0:T(8,128)S(1)}, f32[256,8,8192]{2,0,1:T(8,128)}) fusion(pred[256,8192]{1,0:T(8,128)(4,1)S(1)} %fusion.7, bf16[8192,128]{1,0:T(8,128)(2,1)} %get-tuple-element.35, bf16[256,1024]{1,0:T(8,128)(2,1)S(1)} %gather_fusion, bf16[256,1024]{1,0:T(8,128)(2,1)} %get-tuple-element.42, pred[256]{0:T(512)(128)(4,1)S(1)} %get-tuple-element.31), kind=kOutput, calls=%fused_computation.11 | convolution fusion | flops 4345559040 | bytes 72360192 | tf_op jit(solution)/shard_map/cond/branch_1_fun/qhgd,khd->hgqk/dot_general | solution.py:18
  198.8 26.2 %fusion.16 = f32[1,8,256,128]{3,2,1,0:T(8,128)} fusion(bf16[8192,128]{1,0:T(8,128)(2,1)} %get-tuple-element.36, f32[256,8,8192]{2,0,1:T(8,128)} %get-tuple-element.49, f32[8,256]{1,0:T(8,128)S(1)} %get-tuple-element.47, pred[256,8192]{1,0:T(8,128)(4,1)S(1)} %fusion.7, f32[8,256]{1,0:T(8,128)S(1)} %get-tuple-element.46), kind=kOutput, calls=%fused_computation.21 | convolution fusion | flops 4362338304 | bytes 72368128 | tf_op jit(solution)/shard_map/cond/branch_1_fun/hgqk,khd->hgqd/dot_general | solution.py:34
  225.0 21.8 %fusion.1 = f32[8,256]{1,0:T(8,128)S(1)} fusion(f32[256,8,8192]{2,0,1:T(8,128)} %get-tuple-element.49, f32[8,256]{1,0:T(8,128)S(1)} %get-tuple-element.47, pred[256,8192]{1,0:T(8,128)(4,1)S(1)} %fusion.7), kind=kLoop, calls=%fused_computation.10 | loop fusion | flops 67106816 | bytes 69222400 | tf_op jit(solution)/shard_map/cond/branch_1_fun/reduce_sum | solution.py:33
  246.8 2.6 copy.34
  249.3 1.3 divide_convert_fusion
  250.7 7.1 %convolution_convert_fusion = bf16[256,4096]{1,0:T(8,128)(2,1)} fusion(bf16[256,1024]{0,1:T(8,128)(2,1)S(1)} %bitcast.99, bf16[1024,4096]{1,0:T(8,128)(2,1)} %param.19), kind=kOutput, calls=%fused_computation.37 | convolution fusion | flops 2148532224 | bytes 11010048 | tf_op jit(solution)/shard_map/dot_general | solution.py:125
  257.8 42.7 %reduce-scatter.2.cloned.1.call-done = bf16[32,4096]{1,0:T(8,128)(2,1)} async-done(((bf16[256,4096]{1,0:T(8,128)(2,1)}), bf16[32,4096]{1,0:T(8,128)(2,1)}) %reduce-scatter.2.cloned.1.call-update) | async-done | bytes 262160 | tf_op jit(solution)/shard_map/reduce_scatter | solution.py:124
  (43 shorter events, 9.3 us)
Async XLA Ops:
  6.5 63.9 %copy-start = (bf16[256,1024]{1,0:T(8,128)(2,1)S(1)}, bf16[256,1024]{1,0:T(8,128)(2,1)}, u32[]{:S(2)}) copy-start(bf16[256,1024]{1,0:T(8,128)(2,1)} %param.14) | copy-start | bytes 1572868
  41.9 14.0 %all-to-all-start.2 = ((bf16[32,8,128]{2,1,0:T(8,128)(2,1)}), bf16[32,8,128]{2,1,0:T(8,128)(2,1)S(1)}, u32[]{:S(2)}, u32[]{:S(2)}) async-start(bf16[32,8,128]{2,1,0:T(8,128)(2,1)} %bitcast.22), calls=%async_computation.2 | async-start | bytes 131072 | tf_op jit(solution)/shard_map/all_to_all | solution.py:69
  55.8 11.4 %all-to-all-start.1 = ((bf16[32,8,128]{2,1,0:T(8,128)(2,1)}), bf16[32,8,128]{2,1,0:T(8,128)(2,1)S(1)}, u32[]{:S(2)}, u32[]{:S(2)}) async-start(bf16[32,8,128]{2,1,0:T(8,128)(2,1)} %bitcast.20), calls=%async_computation.1 | async-start | bytes 131072 | tf_op jit(solution)/shard_map/all_to_all | solution.py:68
  60.8 58.3 %all-gather.5.cloned.1.call-start = ((), (), s32[]{:S(2)}) async-start(), calls=%async_computation.5 | async-start | bytes 2162688 | tf_op jit(solution)/shard_map/all_gather | solution.py:103
  69.7 100.0 %all-gather.3.cloned.1.call-start = ((), (), s32[]{:S(2)}) async-start(), calls=%async_computation.4 | async-start | bytes 2162688 | tf_op jit(solution)/shard_map/all_gather | solution.py:102
  72.4 14.9 %all-to-all-start = ((bf16[32,8,1024]{2,1,0:T(8,128)(2,1)}), bf16[32,8,1024]{2,1,0:T(8,128)(2,1)S(1)}, u32[]{:S(2)}, u32[]{:S(2)}) async-start(bf16[32,8,1024]{2,1,0:T(8,128)(2,1)} %bitcast.16), calls=%async_computation | async-start | bytes 1048576 | tf_op jit(solution)/shard_map/all_to_all | solution.py:67
  77.5 223.0 %reduce-scatter.2.cloned.1.call-start = ((), (), s32[]{:S(2)}) async-start(), calls=%async_computation.6 | async-start | bytes 2359296 | tf_op jit(solution)/shard_map/reduce_scatter | solution.py:124
Sparse Core Ops, SparseCore 0:
  69.8 49.2 all-gather.4
  121.7 47.9 all-gather.2
  257.9 42.5 reduce-scatter.1
where the time goes:
time: 308 us; the launch traced here: 307 us
  waiting for transfers between devices  139 us (45%)
  matrix products  59.1 us (19%)
  local copies, waits for them, and re-layouts  44.7 us (15%)
  other arithmetic  31.7 us (10%)
  starting transfers between devices  17.7 us (6%)
  between operations  15.3 us (5%)
    all_gather x1, waiting for transfers between devices, per_device(): lax.all_gather(key_rows, 'ctx', axis=0, tiled=True)  50.6 us
    reduce_scatter x1, waiting for transfers between devices, per_device(): lax.psum_scatter(jnp.dot(attended, out_weight, preferred_element_type=jnp...  42.7 us
    all_gather x1, waiting for transfers between devices, per_device(): lax.all_gather(value_rows, 'ctx', axis=0, tiled=True)  31.8 us
    scatter x1, local copies, waits for them, and re-layouts, per_device(): send_table = jnp.zeros((ctx_size * slot_cap,), jnp.int32).at[slot_index.r...  30.4 us
    dot_general x1, matrix products, attend_block(): jnp.einsum('hgqk,khd->hgqd', weights.astype(jnp.bfloat16), value_heads, p...  26.2 us
    dot_general x1, matrix products, attend_block(): jnp.einsum('qhgd,khd->hgqk', grouped, key_heads, preferred_element_type=j...  25.8 us
    reduce_sum x1, other arithmetic, attend_block(): row_sum = row_sum * rescale + jnp.sum(weights, axis=-1)  21.8 us
    all_to_all x1, starting transfers between devices, per_device(): lax.all_to_all(send_values, 'ctx', split_axis=0, concat_axis=0, tiled=True)  7.62 us
  transfers between devices with their start and end apart: 6, of which 6 were waited for; matrix products, arithmetic and copies ran while one was open for 3% of the time, Pallas kernels for 0%

commit v1 on v0

--- a/solution.py
+++ b/solution.py
@@ -99,7 +99,9 @@
         jnp.zeros((kv_heads, group_size, local_rows, HD), jnp.float32),
     )
     pieces = (
-        lax.all_gather(key_rows, "ctx", axis=0, tiled=True),
+        jnp.concatenate(
+            lax.all_to_all(jnp.stack([key_rows] * lax.axis_size("ctx")), "ctx", 0, 0), axis=0
+        ),
         lax.all_gather(value_rows, "ctx", axis=0, tiled=True),
     )
     first_row = jnp.int32(0)

time: 308 us -> 268 us (0.87)
  waiting for transfers between devices: 139 us -> 81.2 us
  blocking collectives: 0 us -> 14.3 us
    all_gather x1 -> x0, waiting for transfers between devices: 50.6 us -> none  [per_device(): lax.all_gather(key_rows, 'ctx', axis=0, tiled=True)]
    all_gather x1, waiting for transfers between devices: 31.8 us -> 5.46 us  [per_device(): lax.all_gather(value_rows, 'ctx', axis=0, tiled=True)]
    all_to_all x1, waiting for transfers between devices: 4.82 us -> 23.8 us  [per_device(): lax.all_to_all(jnp.stack([key_rows] * lax.axis_size('ctx')), 'ctx', 0, 0)]
    all_to_all x0 -> x1, blocking collectives: none -> 14.3 us  [per_device(): lax.all_to_all(send_queries, 'ctx', split_axis=0, concat_axis=0, tiled=True)]
  transfers between devices with their start and end apart: 6 -> 5, of which waited for: 6 -> 5; matrix products, arithmetic and copies ran while one was open for 3% -> 4% of each run, Pallas kernels for 0% -> 0%
where the time goes in v1:
time: 268 us; the launch traced here: 267 us
  waiting for transfers between devices  81.2 us (30%)
  matrix products  60.3 us (22%)
  local copies, waits for them, and re-layouts  46.4 us (17%)
  other arithmetic  31.6 us (12%)
  starting transfers between devices  18.1 us (7%)
  between operations  15.4 us (6%)
  blocking collectives  14.3 us (5%)
    reduce_scatter x1, waiting for transfers between devices, per_device(): lax.psum_scatter(jnp.dot(attended, out_weight, preferred_element_type=jnp...  44.1 us
    scatter x1, local copies, waits for them, and re-layouts, per_device(): send_table = jnp.zeros((ctx_size * slot_cap,), jnp.int32).at[slot_index.r...  30.4 us
    dot_general x1, matrix products, attend_block(): jnp.einsum('qhgd,khd->hgqk', grouped, key_heads, preferred_element_type=j...  26.9 us
    dot_general x1, matrix products, attend_block(): jnp.einsum('hgqk,khd->hgqd', weights.astype(jnp.bfloat16), value_heads, p...  26.3 us
    all_to_all x1, waiting for transfers between devices, per_device(): lax.all_to_all(jnp.stack([key_rows] * lax.axis_size('ctx')), 'ctx', 0, 0)  23.8 us
    reduce_sum x1, other arithmetic, attend_block(): row_sum = row_sum * rescale + jnp.sum(weights, axis=-1)  21.8 us
    all_to_all x1, blocking collectives, per_device(): lax.all_to_all(send_queries, 'ctx', split_axis=0, concat_axis=0, tiled=True)  14.3 us
    all_to_all x1, starting transfers between devices, per_device(): lax.all_to_all(send_values, 'ctx', split_axis=0, concat_axis=0, tiled=True)  7.62 us
  transfers between devices with their start and end apart: 5, of which 5 were waited for; matrix products, arithmetic and copies ran while one was open for 4% of the time, Pallas kernels for 0%

profile of v1, /device:TPU:2, one launch (start us, length us, event | category | flops | bytes accessed | tf_op | source)
XLA Modules:
  0.0 267.4 jit_solution(4946922148047427218)
XLA Ops:
  9.2 30.4 %scatter_custom_fusion = s32[256]{0:T(256)S(1)} fusion(s32[8192]{0:T(1024)S(1)} %get-tuple-element.51, s32[8192]{0:T(1024)S(1)} %get-tuple-element.50, s32[]{:T(128)} %constant.69.clone.1), kind=kCustom, calls=%fused_computation.89 | custom fusion | bytes 1028 | tf_op jit(solution)/shard_map/scatter | solution.py:61
  39.7 2.2 gather_fusion.4
  41.9 7.6 %all-to-all-start.3 = ((bf16[32,8,128]{2,1,0:T(8,128)(2,1)}), bf16[32,8,128]{2,1,0:T(8,128)(2,1)S(1)}, u32[]{:S(2)}, u32[]{:S(2)}) async-start(bf16[32,8,128]{2,1,0:T(8,128)(2,1)} %bitcast.23), calls=%async_computation.3 | async-start | bytes 131072 | tf_op jit(solution)/shard_map/all_to_all | solution.py:69
  51.2 2.2 gather_fusion.2
  53.4 2.4 all-to-all-done.3
  55.8 5.0 %all-to-all-start.1 = ((bf16[32,8,128]{2,1,0:T(8,128)(2,1)}), bf16[32,8,128]{2,1,0:T(8,128)(2,1)S(1)}, u32[]{:S(2)}, u32[]{:S(2)}) async-start(bf16[32,8,128]{2,1,0:T(8,128)(2,1)} %bitcast.21), calls=%async_computation.1 | async-start | bytes 131072 | tf_op jit(solution)/shard_map/all_to_all | solution.py:68
  61.7 5.5 %all-to-all-done.1 = bf16[32,8,128]{2,1,0:T(8,128)(2,1)S(1)} async-done(((bf16[32,8,128]{2,1,0:T(8,128)(2,1)}), bf16[32,8,128]{2,1,0:T(8,128)(2,1)S(1)}, u32[]{:S(2)}, u32[]{:S(2)}) %all-to-all-start.1) | async-done | bytes 65568 | tf_op jit(solution)/shard_map/all_to_all | solution.py:68
  68.1 1.6 broadcast_select_fusion
  69.7 1.2 gather_fusion.1
  70.9 14.3 %all_to_all.20 = bf16[32,8,1024]{2,1,0:T(8,128)(2,1)S(1)} all-to-all(bf16[32,8,1024]{2,1,0:T(8,128)(2,1)S(1)} %bitcast.99), channel_id=1, replica_groups=mesh['ctx'=32,'head'=8] {'ctx'}, dimensions={0} | all-to-all | bytes 1048576 | tf_op jit(solution)/shard_map/all_to_all | solution.py:67
  85.2 1.8 stack.2
  87.0 5.4 %all-to-all-start.2 = ((bf16[32,256,128]{2,1,0:T(8,128)(2,1)}), bf16[32,256,128]{2,1,0:T(8,128)(2,1)S(1)}, u32[]{:S(2)}, u32[]{:S(2)}) async-start(bf16[32,256,128]{2,1,0:T(8,128)(2,1)} %stack.2), calls=%async_computation.2 | async-start | bytes 4194304 | tf_op jit(solution)/shard_map/all_to_all | solution.py:103
  97.2 23.8 %all-to-all-done.2 = bf16[32,256,128]{2,1,0:T(8,128)(2,1)S(1)} async-done(((bf16[32,256,128]{2,1,0:T(8,128)(2,1)}), bf16[32,256,128]{2,1,0:T(8,128)(2,1)S(1)}, u32[]{:S(2)}, u32[]{:S(2)}) %all-to-all-start.2) | async-done | bytes 2097184 | tf_op jit(solution)/shard_map/all_to_all | solution.py:103
  120.9 5.5 %all-gather.2.cloned.1.call-done = bf16[8192,128]{1,0:T(8,128)(2,1)} async-done(((bf16[256,128]{1,0:T(8,128)(2,1)}), bf16[8192,128]{1,0:T(8,128)(2,1)}) %all-gather.2.cloned.1.call-update) | async-done | bytes 2097168 | tf_op jit(solution)/shard_map/all_gather | solution.py:105
  126.4 81.7 %conditional.1 = (f32[1,8,256]{2,1,0:T(8,128)S(1)}, f32[1,8,256,128]{2,3,1,0:T(8,128)}) conditional(s32[]{:T(128)} %convert_element_type.43, () %tuple.13, (s32[256]{0:T(256)S(1)}, s32[256]{0:T(256)S(1)}, s32[32]{0:T(128)S(1)}, pred[256]{0:T(512)(128)(4,1)S(1)}, bf16[32,8,1024]{2,1,0:T(8,128)(2,1)S(1)}, /*index=5*/s32[256,1]{0,1:T(1,128)S(1)}, ...), branch_computations={%region_9.10_spmd, %region_10.14_spmd} | conditional | flops 8782093312 | bytes 227705264 | solution.py:118
  126.4 2.0 gather_fusion
  128.6 1.9 fusion.7
  130.5 26.9 %fusion.2 = (f32[8,256]{1,0:T(8,128)S(1)}, f32[256,8,8192]{2,0,1:T(8,128)}) fusion(pred[256,8192]{1,0:T(8,128)(4,1)S(1)} %fusion.7, bf16[8192,128,1]{1,0,2:T(8,128)(2,1)} %bitcast.100, bf16[256,1024]{1,0:T(8,128)(2,1)} %gather_fusion, bf16[256,1024]{1,0:T(8,128)(2,1)} %get-tuple-element.42, pred[256]{0:T(512)(128)(4,1)S(1)} %get-tuple-element.31), kind=kOutput, calls=%fused_computation.11 | convolution fusion | flops 4345559040 | bytes 72360192 | tf_op jit(solution)/shard_map/cond/branch_1_fun/qhgd,khd->hgqk/dot_general | solution.py:18
  157.4 26.3 %fusion.14 = f32[1,8,256,128]{3,2,1,0:T(8,128)} fusion(bf16[8192,128]{1,0:T(8,128)(2,1)} %get-tuple-element.36, f32[256,8,8192]{2,0,1:T(8,128)} %get-tuple-element.49, f32[8,256]{1,0:T(8,128)S(1)} %get-tuple-element.47, pred[256,8192]{1,0:T(8,128)(4,1)S(1)} %fusion.7, f32[8,256]{1,0:T(8,128)S(1)} %get-tuple-element.46), kind=kOutput, calls=%fused_computation.19 | convolution fusion | flops 4362338304 | bytes 72368128 | tf_op jit(solution)/shard_map/cond/branch_1_fun/hgqk,khd->hgqd/dot_general | solution.py:34
  183.7 21.8 %fusion.1 = f32[8,256]{1,0:T(8,128)S(1)} fusion(f32[256,8,8192]{2,0,1:T(8,128)} %get-tuple-element.49, f32[8,256]{1,0:T(8,128)S(1)} %get-tuple-element.47, pred[256,8192]{1,0:T(8,128)(4,1)S(1)} %fusion.7), kind=kLoop, calls=%fused_computation.10 | loop fusion | flops 67106816 | bytes 69222400 | tf_op jit(solution)/shard_map/cond/branch_1_fun/reduce_sum | solution.py:33
  205.5 2.6 copy.34
  208.0 1.3 divide_convert_fusion
  209.4 7.1 %convolution_convert_fusion = bf16[256,4096]{1,0:T(8,128)(2,1)} fusion(bf16[256,1024]{0,1:T(8,128)(2,1)S(1)} %bitcast.98, bf16[1024,4096]{1,0:T(8,128)(2,1)} %param.19), kind=kOutput, calls=%fused_computation.36 | convolution fusion | flops 2148532224 | bytes 11010048 | tf_op jit(solution)/shard_map/dot_general | solution.py:127
  216.5 44.1 %reduce-scatter.2.cloned.1.call-done = bf16[32,4096]{1,0:T(8,128)(2,1)} async-done(((bf16[256,4096]{1,0:T(8,128)(2,1)}), bf16[32,4096]{1,0:T(8,128)(2,1)}) %reduce-scatter.2.cloned.1.call-update) | async-done | bytes 262160 | tf_op jit(solution)/shard_map/reduce_scatter | solution.py:126
  (44 shorter events, 9.2 us)
Async XLA Ops:
  6.5 63.2 %copy-start = (bf16[256,1024]{1,0:T(8,128)(2,1)S(1)}, bf16[256,1024]{1,0:T(8,128)(2,1)}, u32[]{:S(2)}) copy-start(bf16[256,1024]{1,0:T(8,128)(2,1)} %param.14) | copy-start | bytes 1572868
  41.9 14.0 %all-to-all-start.3 = ((bf16[32,8,128]{2,1,0:T(8,128)(2,1)}), bf16[32,8,128]{2,1,0:T(8,128)(2,1)S(1)}, u32[]{:S(2)}, u32[]{:S(2)}) async-start(bf16[32,8,128]{2,1,0:T(8,128)(2,1)} %bitcast.23), calls=%async_computation.3 | async-start | bytes 131072 | tf_op jit(solution)/shard_map/all_to_all | solution.py:69
  55.8 11.4 %all-to-all-start.1 = ((bf16[32,8,128]{2,1,0:T(8,128)(2,1)}), bf16[32,8,128]{2,1,0:T(8,128)(2,1)S(1)}, u32[]{:S(2)}, u32[]{:S(2)}) async-start(bf16[32,8,128]{2,1,0:T(8,128)(2,1)} %bitcast.21), calls=%async_computation.1 | async-start | bytes 131072 | tf_op jit(solution)/shard_map/all_to_all | solution.py:68
  60.8 65.6 %all-gather.2.cloned.1.call-start = ((), (), s32[]{:S(2)}) async-start(), calls=%async_computation.5 | async-start | bytes 2162688 | tf_op jit(solution)/shard_map/all_gather | solution.py:105
  87.0 33.9 %all-to-all-start.2 = ((bf16[32,256,128]{2,1,0:T(8,128)(2,1)}), bf16[32,256,128]{2,1,0:T(8,128)(2,1)S(1)}, u32[]{:S(2)}, u32[]{:S(2)}) async-start(bf16[32,256,128]{2,1,0:T(8,128)(2,1)} %stack.2), calls=%async_computation.2 | async-start | bytes 4194304 | tf_op jit(solution)/shard_map/all_to_all | solution.py:103
  92.5 168.1 %reduce-scatter.2.cloned.1.call-start = ((), (), s32[]{:S(2)}) async-start(), calls=%async_computation.6 | async-start | bytes 2359296 | tf_op jit(solution)/shard_map/reduce_scatter | solution.py:126
  126.4 2.0 copy-start.1
Sparse Core Ops, SparseCore 0:
  69.8 56.5 all-gather.1
  216.6 43.9 reduce-scatter.1
